TPU v7x, 32 devices: a whole 2x2x4 slice. The times are simulated.
32 devices in a mesh: doc: 4 (over y, x), cen: 8 (over z, core).
Axes of the slice: x: 2, y: 2, z: 4, core: 2. Of those that a mesh axis runs over, the one named last changes fastest.
Arguments:
- passages: bfloat16 [1536, 1024], P(('doc', 'cen')), may hold values from -64 to 64
- centroids: bfloat16 [8192, 1024], P('cen'), may hold values from -64 to 64
Outputs:
- assign: bfloat16 [1536, 8192], P('doc', 'cen')
- masses: float32 [8192], P('cen')
- new_centroids: float32 [8192, 1024], P('cen', 'doc')
All inputs are finite; a program needn't handle non-finite values.
Results may differ from a plain program's by a relative error of at most 0.008.
Values may be sent and summed in bfloat16 or wider, within the bound.
A program may use at most 64 MiB of HBM per device.

v0:
```python
import math

import jax
import jax.numpy as jnp
from jax import lax
from jax.sharding import PartitionSpec as P

ITERS = 3


def row_log_total(shifted):
    local_max = jnp.max(shifted, axis=1)
    peak = lax.pmax(local_max, "cen")
    total = lax.psum(jnp.sum(jnp.exp(shifted - peak[:, None]), axis=1), "cen")
    return peak + jnp.log(total)


def col_log_total(shifted):
    local_max = jnp.max(shifted, axis=0)
    peak = lax.pmax(local_max, "doc")
    total = lax.psum(jnp.sum(jnp.exp(shifted - peak[None, :]), axis=0), "doc")
    return peak + jnp.log(total)


def shards(passages, centroids):
    cen_count = lax.axis_size("cen")
    doc_count = lax.axis_size("doc")
    width = passages.shape[1]
    scale = 1.0 / math.sqrt(width)
    group_rows = lax.all_gather(passages, "cen", axis=0, tiled=True)
    scores = (
        lax.dot_general(
            group_rows, centroids, (((1,), (1,)), ((), ())), preferred_element_type=jnp.float32
        )
        * scale
    )
    local_cols = centroids.shape[0]
    total_cols = local_cols * cen_count
    total_rows = scores.shape[0] * doc_count
    log_column = math.log(total_rows / total_cols)
    col_potential = jnp.zeros((local_cols,), jnp.float32)
    for iteration in range(ITERS):
        row_potential = -row_log_total(scores + col_potential[None, :])
        col_potential = log_column - col_log_total(scores + row_potential[:, None])
    row_potential = -row_log_total(scores + col_potential[None, :])
    weights = jnp.exp(scores + row_potential[:, None] + col_potential[None, :])
    assign = (weights * total_cols).astype(jnp.bfloat16)
    raw_mass = lax.psum(jnp.sum(weights, axis=0), "doc")
    partial_value = lax.dot_general(
        assign, group_rows, (((0,), (0,)), ((), ())), preferred_element_type=jnp.float32
    )
    sums = lax.psum_scatter(
        partial_value.astype(jnp.bfloat16), "doc", scatter_dimension=1, tiled=True
    ).astype(jnp.float32)
    new_centroids = sums / total_cols / raw_mass[:, None]
    masses = raw_mass * total_cols / total_rows
    return (assign, masses, new_centroids)


def solution(mesh):
    in_specs = (P(("doc", "cen"), None), P("cen", None))
    out_specs = (P("doc", "cen"), P("cen"), P("cen", "doc"))
    return jax.shard_map(shards, mesh=mesh, in_specs=in_specs, out_specs=out_specs, check_vma=False)
```

profile of v0, /device:TPU:0, one launch (start us, length us, event | category | flops | bytes accessed | tf_op | source)
XLA Modules:
  0.0 261.0 jit_solution(13473562070455772774)
XLA Ops:
  7.2 17.6 %all_gather.3 = bf16[384,1024]{1,0:T(8,128)(2,1)S(1)} all-gather(bf16[48,1024]{1,0:T(8,128)(2,1)} %param.2), channel_id=1, replica_groups=mesh['doc'=4,'cen'=8] {'cen'}, dimensions={0}, use_global_device_ids=true | all-gather | bytes 884736 | tf_op jit(solution)/shard_map/all_gather | solution.py:30
  24.8 2.2 fusion.1
  27.0 17.0 %pmax.49 = f32[384]{0:T(512)S(1)} all-reduce(f32[384]{0:T(512)S(1)} %get-tuple-element.5), channel_id=1, replica_groups=mesh['doc'=4,'cen'=8] {'cen'}, use_global_device_ids=true, to_apply=%region_1.0 | all-reduce | flops 384 | bytes 3072 | tf_op jit(solution)/shard_map/pmax | solution.py:13
  44.0 1.8 exponential_reduce_fusion.6
  45.8 13.6 %psum.56 = f32[384]{0:T(512)S(1)} all-reduce(f32[384]{0:T(512)S(1)} %exponential_reduce_fusion.6), channel_id=1, replica_groups=mesh['doc'=4,'cen'=8] {'cen'}, use_global_device_ids=true, to_apply=%region_3.0 | all-reduce | flops 384 | bytes 3072 | tf_op jit(solution)/shard_map/psum | solution.py:14
  59.4 1.6 add_reduce_fusion.5
  61.0 9.9 %pmax.50 = f32[1024]{0:T(1024)S(1)} all-reduce(f32[1024]{0:T(1024)S(1)} %add_reduce_fusion.5), channel_id=1, replica_groups=mesh['doc'=4,'cen'=8] {'doc'}, use_global_device_ids=true, to_apply=%region_5.0 | all-reduce | flops 1024 | bytes 8192 | tf_op jit(solution)/shard_map/pmax | solution.py:20
  70.9 1.7 exponential_reduce_fusion.5
  72.7 8.0 %psum.57 = f32[1024]{0:T(1024)S(1)} all-reduce(f32[1024]{0:T(1024)S(1)} %exponential_reduce_fusion.5), channel_id=1, replica_groups=mesh['doc'=4,'cen'=8] {'doc'}, use_global_device_ids=true, to_apply=%region_7.0 | all-reduce | flops 1024 | bytes 8192 | tf_op jit(solution)/shard_map/psum | solution.py:21
  80.7 1.6 add_reduce_fusion.4
  82.3 13.6 %pmax.51 = f32[384]{0:T(512)S(1)} all-reduce(f32[384]{0:T(512)S(1)} %add_reduce_fusion.4), channel_id=1, replica_groups=mesh['doc'=4,'cen'=8] {'cen'}, use_global_device_ids=true, to_apply=%region_9.0 | all-reduce | flops 384 | bytes 3072 | tf_op jit(solution)/shard_map/pmax | solution.py:13
  95.8 1.8 exponential_reduce_fusion.4
  97.7 13.6 %psum.58 = f32[384]{0:T(512)S(1)} all-reduce(f32[384]{0:T(512)S(1)} %exponential_reduce_fusion.4), channel_id=1, replica_groups=mesh['doc'=4,'cen'=8] {'cen'}, use_global_device_ids=true, to_apply=%region_11.0 | all-reduce | flops 384 | bytes 3072 | tf_op jit(solution)/shard_map/psum | solution.py:14
  112.8 9.0 %pmax.52 = f32[1024]{0:T(1024)S(1)} all-reduce(f32[1024]{0:T(1024)S(1)} %add_reduce_fusion.3), channel_id=1, replica_groups=mesh['doc'=4,'cen'=8] {'doc'}, use_global_device_ids=true, to_apply=%region_13.0 | all-reduce | flops 1024 | bytes 8192 | tf_op jit(solution)/shard_map/pmax | solution.py:20
  121.8 1.7 exponential_reduce_fusion.3
  123.6 8.0 %psum.59 = f32[1024]{0:T(1024)S(1)} all-reduce(f32[1024]{0:T(1024)S(1)} %exponential_reduce_fusion.3), channel_id=1, replica_groups=mesh['doc'=4,'cen'=8] {'doc'}, use_global_device_ids=true, to_apply=%region_15.0 | all-reduce | flops 1024 | bytes 8192 | tf_op jit(solution)/shard_map/psum | solution.py:21
  131.6 1.6 add_reduce_fusion.2
  133.2 13.6 %pmax.53 = f32[384]{0:T(512)S(1)} all-reduce(f32[384]{0:T(512)S(1)} %add_reduce_fusion.2), channel_id=1, replica_groups=mesh['doc'=4,'cen'=8] {'cen'}, use_global_device_ids=true, to_apply=%region_17.0 | all-reduce | flops 384 | bytes 3072 | tf_op jit(solution)/shard_map/pmax | solution.py:13
  146.8 1.8 exponential_reduce_fusion.2
  148.6 13.6 %psum.60 = f32[384]{0:T(512)S(1)} all-reduce(f32[384]{0:T(512)S(1)} %exponential_reduce_fusion.2), channel_id=1, replica_groups=mesh['doc'=4,'cen'=8] {'cen'}, use_global_device_ids=true, to_apply=%region_19.0 | all-reduce | flops 384 | bytes 3072 | tf_op jit(solution)/shard_map/psum | solution.py:14
  163.8 9.7 %pmax.54 = f32[1024]{0:T(1024)S(1)} all-reduce(f32[1024]{0:T(1024)S(1)} %add_reduce_fusion.1), channel_id=1, replica_groups=mesh['doc'=4,'cen'=8] {'doc'}, use_global_device_ids=true, to_apply=%region_21.0 | all-reduce | flops 1024 | bytes 8192 | tf_op jit(solution)/shard_map/pmax | solution.py:20
  173.5 1.7 exponential_reduce_fusion.1
  175.3 8.0 %psum.61 = f32[1024]{0:T(1024)S(1)} all-reduce(f32[1024]{0:T(1024)S(1)} %exponential_reduce_fusion.1), channel_id=1, replica_groups=mesh['doc'=4,'cen'=8] {'doc'}, use_global_device_ids=true, to_apply=%region_23.0 | all-reduce | flops 1024 | bytes 8192 | tf_op jit(solution)/shard_map/psum | solution.py:21
  183.4 1.6 add_reduce_fusion
  184.9 13.6 %pmax.55 = f32[384]{0:T(512)S(1)} all-reduce(f32[384]{0:T(512)S(1)} %add_reduce_fusion), channel_id=1, replica_groups=mesh['doc'=4,'cen'=8] {'cen'}, use_global_device_ids=true, to_apply=%region_25.0 | all-reduce | flops 384 | bytes 3072 | tf_op jit(solution)/shard_map/pmax | solution.py:13
  198.5 1.8 exponential_reduce_fusion
  200.3 13.6 %psum.62 = f32[384]{0:T(512)S(1)} all-reduce(f32[384]{0:T(512)S(1)} %exponential_reduce_fusion), channel_id=1, replica_groups=mesh['doc'=4,'cen'=8] {'cen'}, use_global_device_ids=true, to_apply=%region_27.0 | all-reduce | flops 384 | bytes 3072 | tf_op jit(solution)/shard_map/psum | solution.py:14
  213.9 1.8 fusion
  216.7 2.6 %convolution_convert_fusion = bf16[1024,1024]{1,0:T(8,128)(2,1)} fusion(bf16[384,1024]{1,0:T(8,128)(2,1)S(1)} %get-tuple-element.4, bf16[384,1024]{1,0:T(8,128)(2,1)S(1)} %all_gather.3), kind=kOutput, calls=%fused_computation | convolution fusion | flops 806354944 | bytes 3670016 | tf_op jit(solution)/shard_map/dot_general | solution.py:49
  219.3 9.0 %psum.63 = f32[1024]{0:T(1024)S(1)} all-reduce(f32[1024]{0:T(1024)S(1)} %get-tuple-element.3), channel_id=1, replica_groups=mesh['doc'=4,'cen'=8] {'doc'}, use_global_device_ids=true, to_apply=%region_29.0 | all-reduce | flops 1024 | bytes 8192 | tf_op jit(solution)/shard_map/psum | solution.py:48
  229.0 22.9 %reduce-scatter.2.cloned.1.call-done = bf16[1024,256]{1,0:T(8,128)(2,1)} async-done(((bf16[1024,1024]{1,0:T(8,128)(2,1)}), bf16[1024,256]{1,0:T(8,128)(2,1)}) %reduce-scatter.2.cloned.1.call-update) | async-done | bytes 524304 | tf_op jit(solution)/shard_map/reduce_scatter | solution.py:52
  251.9 2.2 multiply_divide_fusion
  (16 shorter events, 4.8 us)
Async XLA Ops:
  7.2 17.6 %copy-start = (bf16[1024,1024]{1,0:T(8,128)(2,1)S(1)}, bf16[1024,1024]{1,0:T(8,128)(2,1)}, u32[]{:S(2)}) copy-start(bf16[1024,1024]{1,0:T(8,128)(2,1)} %param.3) | copy-start | bytes 6291460
  7.2 244.7 %reduce-scatter.2.cloned.1.call-start = ((), (), s32[]{:S(2)}) async-start(), calls=%async_computation.1 | async-start | bytes 2621440 | tf_op jit(solution)/shard_map/reduce_scatter | solution.py:52
  215.8 0.9 copy-start.1
Sparse Core Ops, SparseCore 0:
  219.4 32.4 reduce-scatter.1
where the time goes:
time: 262 us; the launch traced here: 261 us
  blocking collectives  191 us (73%)
  other arithmetic  26.7 us (10%)
  waiting for transfers between devices  23 us (9%)
  between operations  14.1 us (5%)
  matrix products  4.81 us (2%)
    pmax x4, blocking collectives, row_log_total(): peak = lax.pmax(local_max, 'cen')  57.8 us
    psum x4, blocking collectives, row_log_total(): total = lax.psum(jnp.sum(jnp.exp(shifted - peak[:, None]), axis=1), 'cen')  54.4 us
    pmax x3, blocking collectives, col_log_total(): peak = lax.pmax(local_max, 'doc')  28.6 us
    psum x3, blocking collectives, col_log_total(): total = lax.psum(jnp.sum(jnp.exp(shifted - peak[None, :]), axis=0), 'doc')  24.1 us
    reduce_scatter x1, waiting for transfers between devices, shards(): lax.psum_scatter(partial_value.astype(jnp.bfloat16), 'doc', scatter_dimen...  22.9 us
    all_gather x1, blocking collectives, shards(): group_rows = lax.all_gather(passages, 'cen', axis=0, tiled=True)  17.6 us
    psum x1, blocking collectives, shards(): raw_mass = lax.psum(jnp.sum(weights, axis=0), 'doc')  9.04 us
    reduce_sum x4, other arithmetic, row_log_total(): total = lax.psum(jnp.sum(jnp.exp(shifted - peak[:, None]), axis=1), 'cen')  7.19 us
  transfers between devices with their start and end apart: 1, of which 1 were waited for; matrix products, arithmetic and copies ran while one was open for 0% of the time, Pallas kernels for 0%

commit v1 on v0

v1 whole, which is shorter than its diff:
```python
import functools
import math

import jax
import jax.numpy as jnp
from jax import lax
from jax.experimental import pallas as pl
from jax.experimental.pallas import tpu as pltpu
from jax.sharding import PartitionSpec as P

ITERS = 3
MESH = pl.DeviceIdType.MESH
LANES = 128


def kernel(
    nd, nc, p_ref, c_ref, assign_out, mass_out, newc_out,
    rows_v, cent_v, scores, rp_v, tbuf, row_slots, col_slots, mass_slots, assign_v, part_send, part_recv, newc_v,
    load_sem, gs_sem, gr_sem, rs_sem, rr_sem, cs_sem, cr_sem, ms_sem, mr_sem, ps_sem, pr_sem, out_sem,
):
    d = lax.axis_index("doc")
    c = lax.axis_index("cen")
    block, width = p_ref.shape
    cols = c_ref.shape[0]
    rows = nc * block
    feats = width // nd
    total_cols = cols * nc
    total_rows = rows * nd
    scale = 1.0 / math.sqrt(width)
    log_column = math.log(total_rows / total_cols)
    sends = []

    load_p = pltpu.make_async_copy(p_ref, rows_v.at[c], load_sem.at[0])
    load_c = pltpu.make_async_copy(c_ref, cent_v, load_sem.at[1])
    load_p.start()
    load_c.start()

    barrier = pltpu.get_barrier_semaphore()
    for k in range(1, nc):
        pl.semaphore_signal(barrier, inc=1, device_id=(d, lax.rem(c + k, nc)), device_id_type=MESH)
    for k in range(1, nd):
        pl.semaphore_signal(barrier, inc=1, device_id=(lax.rem(d + k, nd), c), device_id_type=MESH)
    pl.semaphore_wait(barrier, nc + nd - 2)
    load_p.wait()

    def push(src, dst, send, recv, where):
        copy = pltpu.make_async_remote_copy(
            src_ref=src, dst_ref=dst, send_sem=send, recv_sem=recv, device_id=where, device_id_type=MESH
        )
        copy.start()
        sends.append(copy)

    def arrive(ref, send, recv):
        pltpu.make_async_remote_copy(
            src_ref=ref, dst_ref=ref, send_sem=send, recv_sem=recv, device_id=(d, c), device_id_type=MESH
        ).wait_recv()

    mate = c + 1 - 2 * lax.rem(c, 2)
    half = nc // 2
    for k in range(1, half):
        push(rows_v.at[c], rows_v.at[c], gs_sem.at[k], gr_sem.at[c], (d, lax.rem(c + 2 * k, nc)))
    push(rows_v.at[c], rows_v.at[c], gs_sem.at[0], gr_sem.at[c], (d, mate))
    order = [k for pair in zip(range(1, half), reversed(range(1, half))) for k in pair][: half - 1]
    for k in order:
        src = lax.rem(c + nc - 2 * k, nc)
        arrive(rows_v.at[src], gs_sem.at[half + k], gr_sem.at[src])
        push(rows_v.at[src], rows_v.at[src], gs_sem.at[half + k], gr_sem.at[src], (d, mate))
    arrive(rows_v.at[mate], gs_sem.at[0], gr_sem.at[mate])
    for k in range(1, half):
        src = lax.rem(mate + nc - 2 * k, nc)
        arrive(rows_v.at[src], gs_sem.at[0], gr_sem.at[src])
    load_c.wait()

    group_rows = rows_v[...].reshape(rows, width)
    tile = min(256, cols)
    for j in range(cols // tile):
        at = slice(j * tile, (j + 1) * tile)
        scores[:, at] = (
            lax.dot_general(
                group_rows, cent_v[at, :], (((1,), (1,)), ((), ())), preferred_element_type=jnp.float32
            )
            * scale
        )

    step_rows = 64
    lane = lax.broadcasted_iota(jnp.int32, (step_rows, LANES), 1)

    def combine(slots, r, n):
        peak = slots[r, 0, 0:1, :]
        for k in range(1, n):
            peak = jnp.maximum(peak, slots[r, k, 0:1, :])
        total = jnp.zeros_like(peak)
        for k in range(n):
            total = total + slots[r, k, 1:2, :] * jnp.exp(slots[r, k, 0:1, :] - peak)
        return peak + jnp.log(total)

    def row_round(r, col_potential):
        @pl.loop(0, rows // step_rows)
        def _(i):
            at = pl.ds(pl.multiple_of(i * step_rows, step_rows), step_rows)
            x = scores[at, :]
            if col_potential is not None:
                x = x + col_potential
            m = jnp.max(x, axis=1, keepdims=True)
            s = jnp.sum(jnp.exp(x - m), axis=1, keepdims=True)
            tbuf[at, :] = jnp.where(lane == 0, m, s)

        row_slots[r, c, :, :] = tbuf[...].T[0:2, :]
        for k in range(1, nc):
            push(row_slots.at[r, c], row_slots.at[r, c], rs_sem.at[r, k], rr_sem.at[r, c], (d, lax.rem(c + k, nc)))
        for k in range(1, nc):
            src = lax.rem(c + nc - k, nc)
            arrive(row_slots.at[r, src], rs_sem.at[r, k], rr_sem.at[r, src])
        row_potential = -combine(row_slots, r, nc)
        rp_v[...] = jnp.broadcast_to(row_potential, (LANES, rows)).T

    def col_round(r):
        for j in range(cols // LANES):
            at = slice(j * LANES, (j + 1) * LANES)
            x = scores[:, at] + rp_v[...]
            m = jnp.max(x, axis=0, keepdims=True)
            s = jnp.sum(jnp.exp(x - m), axis=0, keepdims=True)
            col_slots[r, d, 0:1, at] = m
            col_slots[r, d, 1:2, at] = s
        for k in range(1, nd):
            push(col_slots.at[r, d], col_slots.at[r, d], cs_sem.at[r, k], cr_sem.at[r, d], (lax.rem(d + k, nd), c))
        for k in range(1, nd):
            src = lax.rem(d + nd - k, nd)
            arrive(col_slots.at[r, src], cs_sem.at[r, k], cr_sem.at[r, src])
        return log_column - combine(col_slots, r, nd)

    col_potential = None
    for r in range(ITERS):
        row_round(r, col_potential)
        col_potential = col_round(r)
    row_round(ITERS, col_potential)

    for j in range(cols // LANES):
        at = slice(j * LANES, (j + 1) * LANES)
        w = jnp.exp(scores[:, at] + rp_v[...] + col_potential[:, at])
        mass_slots[d, :, at] = jnp.sum(w, axis=0, keepdims=True)
        assign_v[:, at] = (w * total_cols).astype(jnp.bfloat16)
    assign_copy = pltpu.make_async_copy(assign_v, assign_out, out_sem.at[0])
    assign_copy.start()
    for k in range(1, nd):
        push(mass_slots.at[d], mass_slots.at[d], ms_sem.at[k], mr_sem.at[d], (lax.rem(d + k, nd), c))

    def partial(q):
        r3 = rows_v[:, :, pl.ds(pl.multiple_of(q * feats, feats), feats)].reshape(rows, feats)
        return lax.dot_general(
            assign_v[...], r3, (((0,), (0,)), ((), ())), preferred_element_type=jnp.float32
        ).astype(jnp.bfloat16)

    for k in reversed(range(1, nd)):
        q = lax.rem(d + k, nd)
        part_send[k, :, :] = partial(q)
        push(part_send.at[k], part_recv.at[d], ps_sem.at[k], pr_sem.at[d], (q, c))
    part_recv[d, :, :] = partial(d)

    for k in range(1, nd):
        src = lax.rem(d + nd - k, nd)
        arrive(mass_slots.at[src], ms_sem.at[k], mr_sem.at[src])
    raw_mass = mass_slots[0]
    for k in range(1, nd):
        raw_mass = raw_mass + mass_slots[k]
    mass_out[...] = raw_mass * total_cols / total_rows
    mass_col = jnp.broadcast_to(raw_mass, (LANES, cols)).T

    for k in range(1, nd):
        src = lax.rem(d + nd - k, nd)
        arrive(part_recv.at[src], ps_sem.at[k], pr_sem.at[src])
    for j in range(feats // LANES):
        at = slice(j * LANES, (j + 1) * LANES)
        sums = part_recv[0, :, at].astype(jnp.float32)
        for k in range(1, nd):
            sums = sums + part_recv[k, :, at].astype(jnp.float32)
        newc_v[:, at] = sums / total_cols / mass_col
    newc_copy = pltpu.make_async_copy(newc_v, newc_out, out_sem.at[1])
    newc_copy.start()
    for copy in sends:
        copy.wait_send()
    assign_copy.wait()
    newc_copy.wait()


def shards(nd, nc, passages, centroids):
    block, width = passages.shape
    cols = centroids.shape[0]
    rows = nc * block
    feats = width // nd
    any_spec = pl.BlockSpec(memory_space=pl.ANY)
    dma = pltpu.SemaphoreType.DMA
    f32, bf16 = jnp.float32, jnp.bfloat16
    assign, masses, newc = pl.pallas_call(
        functools.partial(kernel, nd, nc),
        out_shape=(
            jax.ShapeDtypeStruct((rows, cols), bf16),
            jax.ShapeDtypeStruct((1, cols), f32),
            jax.ShapeDtypeStruct((cols, feats), f32),
        ),
        in_specs=[any_spec, any_spec],
        out_specs=(any_spec, pl.BlockSpec(memory_space=pltpu.VMEM), any_spec),
        scratch_shapes=[
            pltpu.VMEM((nc, block, width), bf16),
            pltpu.VMEM((cols, width), bf16),
            pltpu.VMEM((rows, cols), f32),
            pltpu.VMEM((rows, LANES), f32),
            pltpu.VMEM((rows, LANES), f32),
            pltpu.VMEM((ITERS + 1, nc, 2, rows), f32),
            pltpu.VMEM((ITERS, nd, 2, cols), f32),
            pltpu.VMEM((nd, 1, cols), f32),
            pltpu.VMEM((rows, cols), bf16),
            pltpu.VMEM((nd, cols, feats), bf16),
            pltpu.VMEM((nd, cols, feats), bf16),
            pltpu.VMEM((cols, feats), f32),
            dma((2,)),
            dma((nc,)),
            dma((nc,)),
            dma((ITERS + 1, nc)),
            dma((ITERS + 1, nc)),
            dma((ITERS, nd)),
            dma((ITERS, nd)),
            dma((nd,)),
            dma((nd,)),
            dma((nd,)),
            dma((nd,)),
            dma((2,)),
        ],
        compiler_params=pltpu.CompilerParams(
            collective_id=0, has_side_effects=True, vmem_limit_bytes=52 * 1024 * 1024
        ),
    )(passages, centroids)
    return assign, masses.reshape(cols), newc


def solution(mesh):
    nd, nc = mesh.shape["doc"], mesh.shape["cen"]
    in_specs = (P(("doc", "cen"), None), P("cen", None))
    out_specs = (P("doc", "cen"), P("cen"), P("cen", "doc"))
    return jax.shard_map(
        functools.partial(shards, nd, nc), mesh=mesh, in_specs=in_specs, out_specs=out_specs, check_vma=False
    )
```

time: 262 us -> 79.2 us (0.30)
  blocking collectives: 191 us -> 0 us
  Pallas kernels: 0 us -> 75.1 us
  other arithmetic: 26.7 us -> 0 us
  waiting for transfers between devices: 23 us -> 0 us
  between operations: 14.1 us -> 0.65 us
  matrix products: 4.81 us -> 0 us
    psum x8 -> x0, blocking collectives: 87.5 us -> none  [the longest x4 54.4 us: row_log_total(): total = lax.psum(jnp.sum(jnp.exp(shifted - peak[:, None]), axis=1), 'cen')]
    pmax x7 -> x0, blocking collectives: 86.4 us -> none  [the longest x4 57.8 us: row_log_total(): peak = lax.pmax(local_max, 'cen')]
    pallas_call x0 -> x1, Pallas kernels: none -> 75.1 us  [shards(): pl.pallas_call(functools.partial(kernel, nd, nc), out_shape=(jax.ShapeDty...]
    reduce_scatter x1 -> x0, waiting for transfers between devices: 22.9 us -> none  [shards(): lax.psum_scatter(partial_value.astype(jnp.bfloat16), 'doc', scatter_dimen...]
    all_gather x1 -> x0, blocking collectives: 17.6 us -> none  [shards(): group_rows = lax.all_gather(passages, 'cen', axis=0, tiled=True)]
    reduce_sum x8 -> x0, other arithmetic: 14.2 us -> none  [the longest x4 7.19 us: row_log_total(): total = lax.psum(jnp.sum(jnp.exp(shifted - peak[:, None]), axis=1), 'cen')]
    reduce_max x6 -> x0, other arithmetic: 9.55 us -> none  [the longest x3 4.79 us: row_log_total(): local_max = jnp.max(shifted, axis=1)]
    dot_general x2 -> x0, matrix products: 4.81 us -> none  [the longest x1 2.65 us: shards(): lax.dot_general(assign, group_rows, (((0,), (0,)), ((), ())), preferred_e...]
  transfers between devices with their start and end apart: 1 -> 0, of which waited for: 1 -> 0; matrix products, arithmetic and copies ran while one was open for 0% -> 0% of each run, Pallas kernels for 0% -> 0%
where the time goes in v1:
time: 79.2 us; the launch traced here: 79.1 us
  Pallas kernels  75.1 us (95%)
  local copies, waits for them, and re-layouts  3.33 us (4%)
    pallas_call x1, Pallas kernels, shards(): pl.pallas_call(functools.partial(kernel, nd, nc), out_shape=(jax.ShapeDty...  75.1 us
    unnamed x5, local copies, waits for them, and re-layouts  3.33 us

profile of v1, /device:TPU:0, one launch (start us, length us, event | category | flops | bytes accessed | tf_op | source)
XLA Modules:
  0.0 79.1 jit_solution(11673383937200093576)
XLA Ops:
  0.6 0.0 copy-start
  0.6 0.9 %copy-done = bf16[48,1024]{1,0:T(8,128)(2,1)S(1)} copy-done((bf16[48,1024]{1,0:T(8,128)(2,1)S(1)}, bf16[48,1024]{1,0:T(8,128)(2,1)}, u32[]{:S(2)}) %copy-start) | copy-done | bytes 98328
  1.5 75.1 %shard_map.49 = (bf16[384,1024]{1,0:T(8,128)(2,1)S(1)}, f32[1,1024]{1,0:T(1,128)S(1)}, f32[1024,256]{1,0:T(8,128)S(1)}) custom-call(bf16[48,1024]{1,0:T(8,128)(2,1)S(1)} %copy-done, bf16[1024,1024]{1,0:T(8,128)(2,1)} %c_ref.1), custom_call_target="tpu_custom_call" | custom-call | tf_op jit(solution)/shard_map/pallas_call | solution.py:194
  76.6 0.9 %copy.8 = bf16[384,1024]{1,0:T(8,128)(2,1)} copy(bf16[384,1024]{1,0:T(8,128)(2,1)S(1)} %get-tuple-element.12) | data formatting | bytes 1572864
  77.5 0.6 copy.9
  78.1 1.0 %copy.10 = f32[1024,256]{1,0:T(8,128)} copy(f32[1024,256]{1,0:T(8,128)S(1)} %get-tuple-element.14) | data formatting | bytes 2097152
Async XLA Ops:
  0.6 0.9 %copy-start = (bf16[48,1024]{1,0:T(8,128)(2,1)S(1)}, bf16[48,1024]{1,0:T(8,128)(2,1)}, u32[]{:S(2)}) copy-start(bf16[48,1024]{1,0:T(8,128)(2,1)} %p_ref.1) | copy-start | bytes 294916

commit v2 on v1

--- a/solution.py
+++ b/solution.py
@@ -183,6 +183,212 @@
     newc_copy.wait()
 
 
+def wide_kernel(
+    nd, nc, p_ref, c_ref, assign_out, mass_out, newc_out,
+    rows_v, cent_v, scores, rp_v, tbuf, row_slots, col_slots, rp_slots, mass_slots, assign_v, newc_v,
+    load_sem, gs_sem, gr_sem, ds_sem, dr_sem, rs_sem, rr_sem, cs_sem, cr_sem, ps_sem, pr_sem, out_sem,
+):
+    d = lax.axis_index("doc")
+    c = lax.axis_index("cen")
+    block, width = p_ref.shape
+    cols = c_ref.shape[0]
+    rows = nc * block
+    feats = width // nd
+    total_cols = cols * nc
+    total_rows = rows * nd
+    scale = 1.0 / math.sqrt(width)
+    log_column = math.log(total_rows / total_cols)
+    sends = []
+
+    load_p = pltpu.make_async_copy(p_ref, rows_v.at[d, c], load_sem.at[0])
+    load_c = pltpu.make_async_copy(c_ref, cent_v, load_sem.at[1])
+    load_p.start()
+    load_c.start()
+
+    barrier = pltpu.get_barrier_semaphore()
+    for k in range(1, nc):
+        pl.semaphore_signal(barrier, inc=1, device_id=(d, lax.rem(c + k, nc)), device_id_type=MESH)
+    for k in range(1, nd):
+        pl.semaphore_signal(barrier, inc=1, device_id=(lax.rem(d + k, nd), c), device_id_type=MESH)
+    pl.semaphore_wait(barrier, nc + nd - 2)
+    load_p.wait()
+
+    def push(src, dst, send, recv, where):
+        copy = pltpu.make_async_remote_copy(
+            src_ref=src, dst_ref=dst, send_sem=send, recv_sem=recv, device_id=where, device_id_type=MESH
+        )
+        copy.start()
+        sends.append(copy)
+
+    def arrive(ref, send, recv):
+        pltpu.make_async_remote_copy(
+            src_ref=ref, dst_ref=ref, send_sem=send, recv_sem=recv, device_id=(d, c), device_id_type=MESH
+        ).wait_recv()
+
+    mate = c + 1 - 2 * lax.rem(c, 2)
+    half = nc // 2
+
+    def to_docs(b, slot):
+        for k in range(1, nd):
+            push(rows_v.at[d, b], rows_v.at[d, b], ds_sem.at[k, slot], dr_sem.at[d, b], (lax.rem(d + k, nd), c))
+
+    own = rows_v.at[d, c]
+    for k in range(1, half):
+        push(own, own, gs_sem.at[k], gr_sem.at[c], (d, lax.rem(c + 2 * k, nc)))
+    push(own, own, gs_sem.at[0], gr_sem.at[c], (d, mate))
+    to_docs(c, 0)
+    order = [k for pair in zip(range(1, half), reversed(range(1, half))) for k in pair][: half - 1]
+    for k in order:
+        src = lax.rem(c + nc - 2 * k, nc)
+        got = rows_v.at[d, src]
+        arrive(got, gs_sem.at[half + k], gr_sem.at[src])
+        push(got, got, gs_sem.at[half + k], gr_sem.at[src], (d, mate))
+        to_docs(src, k)
+    arrive(rows_v.at[d, mate], gs_sem.at[0], gr_sem.at[mate])
+    for k in range(1, half):
+        src = lax.rem(mate + nc - 2 * k, nc)
+        arrive(rows_v.at[d, src], gs_sem.at[0], gr_sem.at[src])
+    load_c.wait()
+
+    def relay():
+        for k in range(half):
+            b = lax.rem(c + nc - 2 * k, nc)
+            for q in range(1, nd):
+                src = lax.rem(d + nd - q, nd)
+                got = rows_v.at[src, b]
+                arrive(got, ds_sem.at[0, k], dr_sem.at[src, b])
+                push(got, got, ds_sem.at[nd + q, k], dr_sem.at[src, b], (d, mate))
+
+    def arrive_doc(dd):
+        for k in range(half):
+            b = lax.rem(mate + nc - 2 * k, nc)
+            arrive(rows_v.at[dd, b], ds_sem.at[0, k], dr_sem.at[dd, b])
+
+    tile = min(256, cols)
+
+    def score(dd):
+        for j in range(cols // tile):
+            at = slice(j * tile, (j + 1) * tile)
+            scores[dd, :, at] = (
+                lax.dot_general(
+                    rows_v[dd].reshape(rows, width),
+                    cent_v[at, :],
+                    (((1,), (1,)), ((), ())),
+                    preferred_element_type=jnp.float32,
+                )
+                * scale
+            )
+
+    score(d)
+
+    step_rows = 64
+    lane = lax.broadcasted_iota(jnp.int32, (step_rows, LANES), 1)
+
+    def combine(slots, r, n):
+        peak = slots[r, 0, 0:1, :]
+        for k in range(1, n):
+            peak = jnp.maximum(peak, slots[r, k, 0:1, :])
+        total = jnp.zeros_like(peak)
+        for k in range(n):
+            total = total + slots[r, k, 1:2, :] * jnp.exp(slots[r, k, 0:1, :] - peak)
+        return peak + jnp.log(total)
+
+    def row_round(r, col_potential, meanwhile):
+        @pl.loop(0, rows // step_rows)
+        def _(i):
+            at = pl.ds(pl.multiple_of(i * step_rows, step_rows), step_rows)
+            x = scores[d, at, :]
+            if col_potential is not None:
+                x = x + col_potential
+            m = jnp.max(x, axis=1, keepdims=True)
+            s = jnp.sum(jnp.exp(x - m), axis=1, keepdims=True)
+            tbuf[at, :] = jnp.where(lane == 0, m, s)
+
+        row_slots[r, c, :, :] = tbuf[...].T[0:2, :]
+        for k in range(1, nc):
+            push(row_slots.at[r, c], row_slots.at[r, c], rs_sem.at[r, k], rr_sem.at[r, c], (d, lax.rem(c + k, nc)))
+        meanwhile()
+        for k in range(1, nc):
+            src = lax.rem(c + nc - k, nc)
+            arrive(row_slots.at[r, src], rs_sem.at[r, k], rr_sem.at[r, src])
+        row_potential = -combine(row_slots, r, nc)
+        rp_v[...] = jnp.broadcast_to(row_potential, (LANES, rows)).T
+        return row_potential
+
+    def col_round(r, meanwhile):
+        for j in range(cols // LANES):
+            at = slice(j * LANES, (j + 1) * LANES)
+            x = scores[d, :, at] + rp_v[...]
+            m = jnp.max(x, axis=0, keepdims=True)
+            s = jnp.sum(jnp.exp(x - m), axis=0, keepdims=True)
+            col_slots[r, d, 0:1, at] = m
+            col_slots[r, d, 1:2, at] = s
+        for k in range(1, nd):
+            push(col_slots.at[r, d], col_slots.at[r, d], cs_sem.at[r, k], cr_sem.at[r, d], (lax.rem(d + k, nd), c))
+        meanwhile()
+        for k in range(1, nd):
+            src = lax.rem(d + nd - k, nd)
+            arrive(col_slots.at[r, src], cs_sem.at[r, k], cr_sem.at[r, src])
+        return log_column - combine(col_slots, r, nd)
+
+    def score_other(q):
+        dd = lax.rem(d + q, nd)
+        arrive_doc(dd)
+        score(dd)
+
+    work = [lambda: None, lambda: None, relay] + [functools.partial(score_other, q) for q in range(1, nd)]
+    work += [lambda: None] * (2 * ITERS + 1 - len(work))
+    col_potential = None
+    for r in range(ITERS):
+        row_round(r, col_potential, work[2 * r])
+        col_potential = col_round(r, work[2 * r + 1])
+
+    def finish():
+        for extra in work[2 * ITERS :]:
+            extra()
+
+    rp_slots[d] = row_round(ITERS, col_potential, finish)
+    for k in range(1, nd):
+        push(rp_slots.at[d], rp_slots.at[d], ps_sem.at[k], pr_sem.at[d], (lax.rem(d + k, nd), c))
+
+    assign_copy = pltpu.make_async_copy(assign_v.at[d], assign_out, out_sem.at[0])
+    my_feats = pl.ds(pl.multiple_of(d * feats, feats), feats)
+    for k in range(nd):
+        dd = lax.rem(d + k, nd)
+        if k:
+            arrive(rp_slots.at[dd], ps_sem.at[0], pr_sem.at[dd])
+            rp_v[...] = jnp.broadcast_to(rp_slots[dd], (LANES, rows)).T
+        for j in range(cols // LANES):
+            at = slice(j * LANES, (j + 1) * LANES)
+            w = jnp.exp(scores[dd, :, at] + rp_v[...] + col_potential[:, at])
+            mass_slots[dd, :, at] = jnp.sum(w, axis=0, keepdims=True)
+            assign_v[dd, :, at] = (w * total_cols).astype(jnp.bfloat16)
+        if not k:
+            assign_copy.start()
+        part = lax.dot_general(
+            assign_v[dd],
+            rows_v[dd, :, :, my_feats].reshape(rows, feats),
+            (((0,), (0,)), ((), ())),
+            preferred_element_type=jnp.float32,
+        ).astype(jnp.bfloat16).astype(jnp.float32)
+        newc_v[...] = newc_v[...] + part if k else part
+
+    raw_mass = mass_slots[0]
+    for k in range(1, nd):
+        raw_mass = raw_mass + mass_slots[k]
+    mass_out[...] = raw_mass * total_cols / total_rows
+    mass_col = jnp.broadcast_to(raw_mass, (LANES, cols)).T
+    for j in range(feats // LANES):
+        at = slice(j * LANES, (j + 1) * LANES)
+        newc_v[:, at] = newc_v[:, at] / total_cols / mass_col
+    newc_copy = pltpu.make_async_copy(newc_v, newc_out, out_sem.at[1])
+    newc_copy.start()
+    for copy in sends:
+        copy.wait_send()
+    assign_copy.wait()
+    newc_copy.wait()
+
+
 def shards(nd, nc, passages, centroids):
     block, width = passages.shape
     cols = centroids.shape[0]
@@ -191,16 +397,37 @@
     any_spec = pl.BlockSpec(memory_space=pl.ANY)
     dma = pltpu.SemaphoreType.DMA
     f32, bf16 = jnp.float32, jnp.bfloat16
-    assign, masses, newc = pl.pallas_call(
-        functools.partial(kernel, nd, nc),
-        out_shape=(
-            jax.ShapeDtypeStruct((rows, cols), bf16),
-            jax.ShapeDtypeStruct((1, cols), f32),
-            jax.ShapeDtypeStruct((cols, feats), f32),
-        ),
-        in_specs=[any_spec, any_spec],
-        out_specs=(any_spec, pl.BlockSpec(memory_space=pltpu.VMEM), any_spec),
-        scratch_shapes=[
+    wide = nd * rows * cols <= 2**22 and nc % 2 == 0
+    if wide:
+        body = wide_kernel
+        scratch = [
+            pltpu.VMEM((nd, nc, block, width), bf16),
+            pltpu.VMEM((cols, width), bf16),
+            pltpu.VMEM((nd, rows, cols), f32),
+            pltpu.VMEM((rows, LANES), f32),
+            pltpu.VMEM((rows, LANES), f32),
+            pltpu.VMEM((ITERS + 1, nc, 2, rows), f32),
+            pltpu.VMEM((ITERS, nd, 2, cols), f32),
+            pltpu.VMEM((nd, 1, rows), f32),
+            pltpu.VMEM((nd, 1, cols), f32),
+            pltpu.VMEM((nd, rows, cols), bf16),
+            pltpu.VMEM((cols, feats), f32),
+            dma((2,)),
+            dma((nc,)),
+            dma((nc,)),
+            dma((2 * nd, nc // 2)),
+            dma((nd, nc)),
+            dma((ITERS + 1, nc)),
+            dma((ITERS + 1, nc)),
+            dma((ITERS, nd)),
+            dma((ITERS, nd)),
+            dma((nd,)),
+            dma((nd,)),
+            dma((2,)),
+        ]
+    else:
+        body = kernel
+        scratch = [
             pltpu.VMEM((nc, block, width), bf16),
             pltpu.VMEM((cols, width), bf16),
             pltpu.VMEM((rows, cols), f32),
@@ -225,7 +452,17 @@
             dma((nd,)),
             dma((nd,)),
             dma((2,)),
-        ],
+        ]
+    assign, masses, newc = pl.pallas_call(
+        functools.partial(body, nd, nc),
+        out_shape=(
+            jax.ShapeDtypeStruct((rows, cols), bf16),
+            jax.ShapeDtypeStruct((1, cols), f32),
+            jax.ShapeDtypeStruct((cols, feats), f32),
+        ),
+        in_specs=[pl.BlockSpec(memory_space=pltpu.MemorySpace.HBM)] * 2,
+        out_specs=(any_spec, pl.BlockSpec(memory_space=pltpu.VMEM), any_spec),
+        scratch_shapes=scratch,
         compiler_params=pltpu.CompilerParams(
             collective_id=0, has_side_effects=True, vmem_limit_bytes=52 * 1024 * 1024
         ),

time: 79.2 us -> 59.5 us (0.75)
  Pallas kernels: 75.1 us -> 55.3 us
    pallas_call x1, Pallas kernels: 75.1 us -> 55.3 us  [shards(): pl.pallas_call(functools.partial(body, nd, nc), out_shape=(jax.ShapeDtype...]
where the time goes in v2:
time: 59.5 us; the launch traced here: 59.3 us
  Pallas kernels  55.3 us (93%)
  local copies, waits for them, and re-layouts  3.33 us (6%)
  between operations  0.65 us (1%)
    pallas_call x1, Pallas kernels, shards(): pl.pallas_call(functools.partial(body, nd, nc), out_shape=(jax.ShapeDtype...  55.3 us
    unnamed x5, local copies, waits for them, and re-layouts  3.33 us

profile of v2, /device:TPU:0, one launch (start us, length us, event | category | flops | bytes accessed | tf_op | source)
XLA Modules:
  0.0 59.3 jit_solution(11921767161687550015)
XLA Ops:
  0.6 0.0 copy-start
  0.6 0.9 %copy-done = bf16[48,1024]{1,0:T(8,128)(2,1)S(1)} copy-done((bf16[48,1024]{1,0:T(8,128)(2,1)S(1)}, bf16[48,1024]{1,0:T(8,128)(2,1)}, u32[]{:S(2)}) %copy-start) | copy-done | bytes 98328
  1.5 55.3 %shard_map.49 = (bf16[384,1024]{1,0:T(8,128)(2,1)S(1)}, f32[1,1024]{1,0:T(1,128)S(1)}, f32[1024,256]{1,0:T(8,128)S(1)}) custom-call(bf16[48,1024]{1,0:T(8,128)(2,1)S(1)} %copy-done, bf16[1024,1024]{1,0:T(8,128)(2,1)} %c_ref.1), custom_call_target="tpu_custom_call" | custom-call | tf_op jit(solution)/shard_map/pallas_call | solution.py:456
  56.9 0.9 %copy.8 = bf16[384,1024]{1,0:T(8,128)(2,1)} copy(bf16[384,1024]{1,0:T(8,128)(2,1)S(1)} %get-tuple-element.12) | data formatting | bytes 1572864
  57.7 0.6 %copy.9 = f32[1024]{0:T(1024)} copy(f32[1024]{0:T(1024)S(1)} %bitcast.1) | data formatting | bytes 8192
  58.3 1.0 %copy.10 = f32[1024,256]{1,0:T(8,128)} copy(f32[1024,256]{1,0:T(8,128)S(1)} %get-tuple-element.14) | data formatting | bytes 2097152
Async XLA Ops:
  0.6 0.9 %copy-start = (bf16[48,1024]{1,0:T(8,128)(2,1)S(1)}, bf16[48,1024]{1,0:T(8,128)(2,1)}, u32[]{:S(2)}) copy-start(bf16[48,1024]{1,0:T(8,128)(2,1)} %p_ref.1) | copy-start | bytes 294916

commit v3 on v2

--- a/solution.py
+++ b/solution.py
@@ -185,8 +185,8 @@
 
 def wide_kernel(
     nd, nc, p_ref, c_ref, assign_out, mass_out, newc_out,
-    rows_v, cent_v, scores, rp_v, tbuf, row_slots, col_slots, rp_slots, mass_slots, assign_v, newc_v,
-    load_sem, gs_sem, gr_sem, ds_sem, dr_sem, rs_sem, rr_sem, cs_sem, cr_sem, ps_sem, pr_sem, out_sem,
+    rows_v, cent_v, scores, rp_v, tbuf, row_slots, col_slots, peak_v, mass_slots, assign_v, newc_v,
+    load_sem, gs_sem, gr_sem, ds_sem, dr_sem, rs_sem, rr_sem, cs_sem, cr_sem, out_sem,
 ):
     d = lax.axis_index("doc")
     c = lax.axis_index("cen")
@@ -293,27 +293,31 @@
             total = total + slots[r, k, 1:2, :] * jnp.exp(slots[r, k, 0:1, :] - peak)
         return peak + jnp.log(total)
 
-    def row_round(r, col_potential, meanwhile):
+    def row_pass(dd, r, col_potential, keep):
         @pl.loop(0, rows // step_rows)
         def _(i):
             at = pl.ds(pl.multiple_of(i * step_rows, step_rows), step_rows)
-            x = scores[d, at, :]
+            x = scores[dd, at, :]
             if col_potential is not None:
                 x = x + col_potential
             m = jnp.max(x, axis=1, keepdims=True)
-            s = jnp.sum(jnp.exp(x - m), axis=1, keepdims=True)
+            e = jnp.exp(x - m)
+            s = jnp.sum(e, axis=1, keepdims=True)
             tbuf[at, :] = jnp.where(lane == 0, m, s)
+            if keep:
+                scores[dd, at, :] = e
+                peak_v[dd, at, :] = jnp.broadcast_to(m, (step_rows, LANES))
 
         row_slots[r, c, :, :] = tbuf[...].T[0:2, :]
         for k in range(1, nc):
             push(row_slots.at[r, c], row_slots.at[r, c], rs_sem.at[r, k], rr_sem.at[r, c], (d, lax.rem(c + k, nc)))
-        meanwhile()
+
+    def row_finish(r):
         for k in range(1, nc):
             src = lax.rem(c + nc - k, nc)
             arrive(row_slots.at[r, src], rs_sem.at[r, k], rr_sem.at[r, src])
         row_potential = -combine(row_slots, r, nc)
-        rp_v[...] = jnp.broadcast_to(row_potential, (LANES, rows)).T
-        return row_potential
+        return jnp.broadcast_to(row_potential, (LANES, rows)).T
 
     def col_round(r, meanwhile):
         for j in range(cols // LANES):
@@ -337,33 +341,29 @@
         score(dd)
 
     work = [lambda: None, lambda: None, relay] + [functools.partial(score_other, q) for q in range(1, nd)]
-    work += [lambda: None] * (2 * ITERS + 1 - len(work))
+    work += [lambda: None] * (2 * ITERS - len(work))
     col_potential = None
     for r in range(ITERS):
-        row_round(r, col_potential, work[2 * r])
+        row_pass(d, r, col_potential, False)
+        work[2 * r]()
+        rp_v[...] = row_finish(r)
         col_potential = col_round(r, work[2 * r + 1])
-
-    def finish():
-        for extra in work[2 * ITERS :]:
-            extra()
-
-    rp_slots[d] = row_round(ITERS, col_potential, finish)
-    for k in range(1, nd):
-        push(rp_slots.at[d], rp_slots.at[d], ps_sem.at[k], pr_sem.at[d], (lax.rem(d + k, nd), c))
-
+    for extra in work[2 * ITERS :]:
+        extra()
+
+    for q in range(nd):
+        row_pass(lax.rem(d + q, nd), ITERS + q, col_potential, True)
     assign_copy = pltpu.make_async_copy(assign_v.at[d], assign_out, out_sem.at[0])
     my_feats = pl.ds(pl.multiple_of(d * feats, feats), feats)
-    for k in range(nd):
-        dd = lax.rem(d + k, nd)
-        if k:
-            arrive(rp_slots.at[dd], ps_sem.at[0], pr_sem.at[dd])
-            rp_v[...] = jnp.broadcast_to(rp_slots[dd], (LANES, rows)).T
+    for q in range(nd):
+        dd = lax.rem(d + q, nd)
+        rp_v[...] = jnp.exp(peak_v[dd] + row_finish(ITERS + q))
         for j in range(cols // LANES):
             at = slice(j * LANES, (j + 1) * LANES)
-            w = jnp.exp(scores[dd, :, at] + rp_v[...] + col_potential[:, at])
+            w = scores[dd, :, at] * rp_v[...]
             mass_slots[dd, :, at] = jnp.sum(w, axis=0, keepdims=True)
             assign_v[dd, :, at] = (w * total_cols).astype(jnp.bfloat16)
-        if not k:
+        if not q:
             assign_copy.start()
         part = lax.dot_general(
             assign_v[dd],
@@ -371,7 +371,7 @@
             (((0,), (0,)), ((), ())),
             preferred_element_type=jnp.float32,
         ).astype(jnp.bfloat16).astype(jnp.float32)
-        newc_v[...] = newc_v[...] + part if k else part
+        newc_v[...] = newc_v[...] + part if q else part
 
     raw_mass = mass_slots[0]
     for k in range(1, nd):
@@ -400,15 +400,16 @@
     wide = nd * rows * cols <= 2**22 and nc % 2 == 0
     if wide:
         body = wide_kernel
+        limit = 28 * 1024 * 1024
         scratch = [
             pltpu.VMEM((nd, nc, block, width), bf16),
             pltpu.VMEM((cols, width), bf16),
             pltpu.VMEM((nd, rows, cols), f32),
             pltpu.VMEM((rows, LANES), f32),
             pltpu.VMEM((rows, LANES), f32),
-            pltpu.VMEM((ITERS + 1, nc, 2, rows), f32),
+            pltpu.VMEM((ITERS + nd, nc, 2, rows), f32),
             pltpu.VMEM((ITERS, nd, 2, cols), f32),
-            pltpu.VMEM((nd, 1, rows), f32),
+            pltpu.VMEM((nd, rows, LANES), f32),
             pltpu.VMEM((nd, 1, cols), f32),
             pltpu.VMEM((nd, rows, cols), bf16),
             pltpu.VMEM((cols, feats), f32),
@@ -417,16 +418,15 @@
             dma((nc,)),
             dma((2 * nd, nc // 2)),
             dma((nd, nc)),
-            dma((ITERS + 1, nc)),
-            dma((ITERS + 1, nc)),
+            dma((ITERS + nd, nc)),
+            dma((ITERS + nd, nc)),
             dma((ITERS, nd)),
             dma((ITERS, nd)),
-            dma((nd,)),
-            dma((nd,)),
             dma((2,)),
         ]
     else:
         body = kernel
+        limit = 52 * 1024 * 1024
         scratch = [
             pltpu.VMEM((nc, block, width), bf16),
             pltpu.VMEM((cols, width), bf16),
@@ -464,7 +464,7 @@
         out_specs=(any_spec, pl.BlockSpec(memory_space=pltpu.VMEM), any_spec),
         scratch_shapes=scratch,
         compiler_params=pltpu.CompilerParams(
-            collective_id=0, has_side_effects=True, vmem_limit_bytes=52 * 1024 * 1024
+            collective_id=0, has_side_effects=True, vmem_limit_bytes=limit
         ),
     )(passages, centroids)
     return assign, masses.reshape(cols), newc

time: 59.5 us -> 61.2 us (1.029)
  local copies, waits for them, and re-layouts: 3.33 us -> 4.92 us
    unnamed x5 -> x7, local copies, waits for them, and re-layouts: 3.33 us -> 4.92 us
where the time goes in v3:
time: 61.2 us; the launch traced here: 61 us
  Pallas kernels  55.5 us (91%)
  local copies, waits for them, and re-layouts  4.92 us (8%)
  between operations  0.65 us (1%)
    pallas_call x1, Pallas kernels, shards(): pl.pallas_call(functools.partial(body, nd, nc), out_shape=(jax.ShapeDtype...  55.5 us
    unnamed x7, local copies, waits for them, and re-layouts  4.92 us

profile of v3, /device:TPU:0, one launch (start us, length us, event | category | flops | bytes accessed | tf_op | source)
XLA Modules:
  0.0 61.0 jit_solution(10831918034645941630)
XLA Ops:
  0.6 0.0 copy-start
  0.6 1.6 %copy-done = bf16[1024,1024]{1,0:T(8,128)(2,1)S(1)} copy-done((bf16[1024,1024]{1,0:T(8,128)(2,1)S(1)}, bf16[1024,1024]{1,0:T(8,128)(2,1)}, u32[]{:S(2)}) %copy-start) | copy-done | bytes 2097176
  2.2 0.0 copy-start.1
  2.2 0.9 %copy-done.1 = bf16[48,1024]{1,0:T(8,128)(2,1)S(1)} copy-done((bf16[48,1024]{1,0:T(8,128)(2,1)S(1)}, bf16[48,1024]{1,0:T(8,128)(2,1)}, u32[]{:S(2)}) %copy-start.1) | copy-done | bytes 98328
  3.1 55.5 %shard_map.49 = (bf16[384,1024]{1,0:T(8,128)(2,1)S(1)}, f32[1,1024]{1,0:T(1,128)S(1)}, f32[1024,256]{1,0:T(8,128)S(1)}) custom-call(bf16[48,1024]{1,0:T(8,128)(2,1)S(1)} %copy-done.1, bf16[1024,1024]{1,0:T(8,128)(2,1)S(1)} %copy-done), custom_call_target="tpu_custom_call" | custom-call | tf_op jit(solution)/shard_map/pallas_call | solution.py:456
  58.6 0.9 %copy.8 = bf16[384,1024]{1,0:T(8,128)(2,1)} copy(bf16[384,1024]{1,0:T(8,128)(2,1)S(1)} %get-tuple-element.12) | data formatting | bytes 1572864
  59.5 0.6 copy.9
  60.1 1.0 %copy.10 = f32[1024,256]{1,0:T(8,128)} copy(f32[1024,256]{1,0:T(8,128)S(1)} %get-tuple-element.14) | data formatting | bytes 2097152
Async XLA Ops:
  0.6 1.6 %copy-start = (bf16[1024,1024]{1,0:T(8,128)(2,1)S(1)}, bf16[1024,1024]{1,0:T(8,128)(2,1)}, u32[]{:S(2)}) copy-start(bf16[1024,1024]{1,0:T(8,128)(2,1)} %c_ref.1) | copy-start | bytes 6291460
  2.2 0.9 %copy-start.1 = (bf16[48,1024]{1,0:T(8,128)(2,1)S(1)}, bf16[48,1024]{1,0:T(8,128)(2,1)}, u32[]{:S(2)}) copy-start(bf16[48,1024]{1,0:T(8,128)(2,1)} %p_ref.1) | copy-start | bytes 294916

commit v4 on v3

--- a/solution.py
+++ b/solution.py
@@ -185,7 +185,7 @@
 
 def wide_kernel(
     nd, nc, p_ref, c_ref, assign_out, mass_out, newc_out,
-    rows_v, cent_v, scores, rp_v, tbuf, row_slots, col_slots, peak_v, mass_slots, assign_v, newc_v,
+    rows_v, cent_v, scores, rp_v, tbuf, row_slots, col_slots, peak_v, mass_slots, assign_v, sums_v, newc_v,
     load_sem, gs_sem, gr_sem, ds_sem, dr_sem, rs_sem, rr_sem, cs_sem, cr_sem, out_sem,
 ):
     d = lax.axis_index("doc")
@@ -366,21 +366,20 @@
         if not q:
             assign_copy.start()
         part = lax.dot_general(
+            rows_v[dd, :, :, my_feats].reshape(rows, feats),
             assign_v[dd],
-            rows_v[dd, :, :, my_feats].reshape(rows, feats),
             (((0,), (0,)), ((), ())),
             preferred_element_type=jnp.float32,
         ).astype(jnp.bfloat16).astype(jnp.float32)
-        newc_v[...] = newc_v[...] + part if q else part
+        sums_v[...] = sums_v[...] + part if q else part
 
     raw_mass = mass_slots[0]
     for k in range(1, nd):
         raw_mass = raw_mass + mass_slots[k]
     mass_out[...] = raw_mass * total_cols / total_rows
-    mass_col = jnp.broadcast_to(raw_mass, (LANES, cols)).T
-    for j in range(feats // LANES):
+    for j in range(cols // LANES):
         at = slice(j * LANES, (j + 1) * LANES)
-        newc_v[:, at] = newc_v[:, at] / total_cols / mass_col
+        newc_v[at, :] = (sums_v[:, at] / total_cols / raw_mass[:, at]).T
     newc_copy = pltpu.make_async_copy(newc_v, newc_out, out_sem.at[1])
     newc_copy.start()
     for copy in sends:
@@ -400,7 +399,7 @@
     wide = nd * rows * cols <= 2**22 and nc % 2 == 0
     if wide:
         body = wide_kernel
-        limit = 28 * 1024 * 1024
+        limit = 52 * 1024 * 1024
         scratch = [
             pltpu.VMEM((nd, nc, block, width), bf16),
             pltpu.VMEM((cols, width), bf16),
@@ -412,6 +411,7 @@
             pltpu.VMEM((nd, rows, LANES), f32),
             pltpu.VMEM((nd, 1, cols), f32),
             pltpu.VMEM((nd, rows, cols), bf16),
+            pltpu.VMEM((feats, cols), f32),
             pltpu.VMEM((cols, feats), f32),
             dma((2,)),
             dma((nc,)),

time: 61.2 us -> 59.2 us (0.967)
  local copies, waits for them, and re-layouts: 4.92 us -> 3.33 us
    unnamed x7 -> x5, local copies, waits for them, and re-layouts: 4.92 us -> 3.33 us
where the time goes in v4:
time: 59.2 us; the launch traced here: 59 us
  Pallas kernels  55 us (93%)
  local copies, waits for them, and re-layouts  3.33 us (6%)
  between operations  0.65 us (1%)
    pallas_call x1, Pallas kernels, shards(): pl.pallas_call(functools.partial(body, nd, nc), out_shape=(jax.ShapeDtype...  55 us
    unnamed x5, local copies, waits for them, and re-layouts  3.33 us

profile of v4, /device:TPU:0, one launch (start us, length us, event | category | flops | bytes accessed | tf_op | source)
XLA Modules:
  0.0 59.0 jit_solution(11717549427014432568)
XLA Ops:
  0.6 0.0 copy-start
  0.6 0.9 %copy-done = bf16[48,1024]{1,0:T(8,128)(2,1)S(1)} copy-done((bf16[48,1024]{1,0:T(8,128)(2,1)S(1)}, bf16[48,1024]{1,0:T(8,128)(2,1)}, u32[]{:S(2)}) %copy-start) | copy-done | bytes 98328
  1.5 55.0 %shard_map.49 = (bf16[384,1024]{1,0:T(8,128)(2,1)S(1)}, f32[1,1024]{1,0:T(1,128)S(1)}, f32[1024,256]{1,0:T(8,128)S(1)}) custom-call(bf16[48,1024]{1,0:T(8,128)(2,1)S(1)} %copy-done, bf16[1024,1024]{1,0:T(8,128)(2,1)} %c_ref.1), custom_call_target="tpu_custom_call" | custom-call | tf_op jit(solution)/shard_map/pallas_call | solution.py:456
  56.6 0.9 %copy.8 = bf16[384,1024]{1,0:T(8,128)(2,1)} copy(bf16[384,1024]{1,0:T(8,128)(2,1)S(1)} %get-tuple-element.12) | data formatting | bytes 1572864
  57.4 0.6 %copy.9 = f32[1024]{0:T(1024)} copy(f32[1024]{0:T(1024)S(1)} %bitcast.1) | data formatting | bytes 8192
  58.0 1.0 %copy.10 = f32[1024,256]{1,0:T(8,128)} copy(f32[1024,256]{1,0:T(8,128)S(1)} %get-tuple-element.14) | data formatting | bytes 2097152
Async XLA Ops:
  0.6 0.9 %copy-start = (bf16[48,1024]{1,0:T(8,128)(2,1)S(1)}, bf16[48,1024]{1,0:T(8,128)(2,1)}, u32[]{:S(2)}) copy-start(bf16[48,1024]{1,0:T(8,128)(2,1)} %p_ref.1) | copy-start | bytes 294916
